TPU v7x, 256 devices: a whole 4x4x8 slice. The times are simulated.
256 devices in a mesh: dp: 4 (over y), tensor: 64 (over x, z, core).
Axes of the slice: x: 4, y: 4, z: 8, core: 2. Of those that a mesh axis runs over, the one named last changes fastest.
Arguments:
- tokens: bfloat16 [4, 8192, 1536], P('dp', 'tensor'), may hold values from -6 to 6
- attn_gain: float32 [1536], replicated, may hold values from 0.1 to 1.9
- qkv_weight: bfloat16 [1536, 2560], P(None, 'dp'), may hold values from -0.25 to 0.25
- out_weight: bfloat16 [1536, 1536], P('dp'), may hold values from -0.15625 to 0.15625
- prefix_cache: bfloat16 [4, 512, 2, 512], P('dp', 'tensor'), may hold values from -640 to 640
- lengths: int32 [4, 256], P('dp'), may hold values from 1 to 384, 8192 in all within a row
- ffn_gain: float32 [1536], replicated, may hold values from 0.1 to 1.9
- expert_ids: int32 [4, 8192, 8], P('dp', 'tensor'), may hold values from 0 to 31, all different within a row; in each aligned block of 128 rows (0 to 127, 128 to 255, ..., all dimensions but the last counted through in order) at most 40 rows name the same one
- gate_weights: float32 [4, 8192, 8], P('dp', 'tensor'), may hold values from 0.05 to 0.5
- expert_in: bfloat16 [64, 1536, 512], P('tensor'), may hold values from -0.15625 to 0.15625
- expert_out: bfloat16 [64, 256, 1536], P('tensor'), may hold values from -0.25 to 0.25
Outputs:
- hidden_state: bfloat16 [4, 8192, 1536], P('dp', 'tensor')
- mixed: bfloat16 [4, 8192, 1536], P('dp', 'tensor')
Inputs may be any that keep to these rules, and one draw needn't show every extreme that they name: `lengths`: each group's 256 requests fill its 8192 suffix positions in order, and the longest holds exactly 384 tokens. `expert_ids`: each token names 8 different experts; among the 128 tokens of one device no expert is named more than 40 times, a bound that some block reaches.
All inputs are finite; a program needn't handle non-finite values.
Results may differ from a plain program's by a relative error of at most 0.014.
The roundings to bfloat16 on the way count: a program that leaves them out, or rounds other values in their place, can miss the bound.
Values may be sent and summed in bfloat16 or wider, within the bound.
No kernel may reach another device: no remote copies, remote signals or barrier semaphores. Data moves between devices by JAX's collectives and lax.ppermute only.
A program may use at most 128 MiB of HBM per device.

v0:
```python
import jax
import jax.numpy as jnp
from jax import lax
from jax.sharding import PartitionSpec as P

HEADS = 24
KV_HEADS = 8
HEAD_DIM = 64
EXPERTS = 32
TOPK = 8
SHIFTS = 2
CAP = 40
EPS = 1e-06
THETA = 10000.0


def from_behind(value, axis, steps):
    count = lax.axis_size(axis)
    first, last = (max(0, -steps), min(count, count - steps))
    return lax.ppermute(value, axis, [(source, source + steps) for source in range(first, last)])


def rms_norm(x, gain):
    values = x.astype(jnp.float32)
    mean_sq = jnp.mean(values * values, axis=-1, keepdims=True)
    return (values * lax.rsqrt(mean_sq + EPS) * gain).astype(jnp.bfloat16)


def rotary(x, positions):
    half = x.shape[-1] // 2
    freqs = THETA ** (-jnp.arange(half, dtype=jnp.float32) * 2.0 / x.shape[-1])
    angles = positions.astype(jnp.float32)[:, None] * freqs[None, :]
    cosine = jnp.concatenate([jnp.cos(angles), jnp.cos(angles)], axis=-1)[:, None, :]
    sine = jnp.concatenate([jnp.sin(angles), jnp.sin(angles)], axis=-1)[:, None, :]
    turned = jnp.concatenate([-x[..., half:], x[..., :half]], axis=-1)
    return x * cosine + turned * sine


def request_info(index, lengths):
    ends = jnp.cumsum(lengths, dtype=jnp.int32)
    before = ends[None, :] <= index[:, None]
    segment = jnp.sum(before.astype(jnp.int32), axis=1, dtype=jnp.int32)
    start = jnp.sum(jnp.where(before, lengths[None, :], 0), axis=1, dtype=jnp.int32)
    return (segment, index - start)


def merge_block(carry, scores, values, visible):
    best, total, acc = carry
    if visible is not None:
        scores = jnp.where(visible, scores, -1e30)
    newest = jnp.maximum(best, jnp.max(scores, axis=-1))
    probs = jnp.exp(scores - newest[..., None])
    if visible is not None:
        probs = jnp.where(visible, probs, 0.0)
    decay = jnp.exp(best - newest)
    total = total * decay + jnp.sum(probs, axis=-1)
    acc = acc * decay[..., None] + jnp.einsum(
        "tgrn,ngd->tgrd", probs.astype(jnp.bfloat16), values, preferred_element_type=jnp.float32
    )
    return (newest, total, acc)


def shards(
    tokens,
    attn_gain,
    qkv_weight,
    out_weight,
    prefix_cache,
    lengths,
    ffn_gain,
    expert_ids,
    gate_weights,
    expert_in,
    expert_out,
):
    rows = tokens.shape[1]
    model = tokens.shape[2]
    head_cols = HEADS * HEAD_DIM
    kv_cols = KV_HEADS * HEAD_DIM
    ratio = HEADS // KV_HEADS
    scale = 1.0 / HEAD_DIM**0.5
    lanes = lax.axis_size("tensor")
    prefix_len = prefix_cache.shape[1] * lanes
    own_lengths = lengths[0]
    inputs = tokens[0]
    normed = rms_norm(inputs, attn_gain)
    full_qkv, full_out = (
        lax.all_gather(qkv_weight, "dp", axis=1, tiled=True),
        lax.all_gather(out_weight, "dp", axis=0, tiled=True),
    )
    qkv = jnp.dot(normed, full_qkv, preferred_element_type=jnp.float32).astype(jnp.bfloat16)
    lane = lax.axis_index("tensor")
    q_index = lane * rows + jnp.arange(rows, dtype=jnp.int32)
    q_segment, offset = request_info(q_index, own_lengths)
    positions = prefix_len + offset
    query = rotary(
        qkv[:, :head_cols].astype(jnp.float32).reshape(rows, HEADS, HEAD_DIM), positions
    ).astype(jnp.bfloat16)
    query = query.reshape(rows, KV_HEADS, ratio, HEAD_DIM)
    keys = rotary(
        qkv[:, head_cols : head_cols + kv_cols]
        .astype(jnp.float32)
        .reshape(rows, KV_HEADS, HEAD_DIM),
        positions,
    ).astype(jnp.bfloat16)
    local_pairs = jnp.stack([keys.reshape(rows, kv_cols), qkv[:, head_cols + kv_cols :]], axis=1)
    start_carry = (
        jnp.full((rows, KV_HEADS, ratio), -1e30, jnp.float32),
        jnp.zeros((rows, KV_HEADS, ratio), jnp.float32),
        jnp.zeros((rows, KV_HEADS, ratio, HEAD_DIM), jnp.float32),
    )
    piece = lax.all_gather(prefix_cache[0], "tensor", axis=0, tiled=True)
    count = piece.shape[0]
    cached_keys = piece[:, 0].reshape(count, KV_HEADS, HEAD_DIM)
    cached_values = piece[:, 1].reshape(count, KV_HEADS, HEAD_DIM)
    scores = (
        jnp.einsum("tgrd,ngd->tgrn", query, cached_keys, preferred_element_type=jnp.float32) * scale
    )
    carry = merge_block(start_carry, scores, cached_values, None)
    window = local_pairs[None]
    for bit in range(SHIFTS):
        earlier = from_behind(window, "tensor", 2**bit)
        window = jnp.concatenate([window, earlier], axis=0)
    depth = window.shape[0]
    k_index = (
        (lane - jnp.arange(depth, dtype=jnp.int32))[:, None] * rows
        + jnp.arange(rows, dtype=jnp.int32)[None, :]
    ).reshape(-1)
    k_segment, unused = request_info(k_index, own_lengths)
    visible = (
        (k_index[None, :] >= 0)
        & (k_index[None, :] <= q_index[:, None])
        & (k_segment[None, :] == q_segment[:, None])
    )
    suffix_pairs = window.reshape(depth * rows, 2, kv_cols)
    suffix_keys = suffix_pairs[:, 0].reshape(depth * rows, KV_HEADS, HEAD_DIM)
    suffix_values = suffix_pairs[:, 1].reshape(depth * rows, KV_HEADS, HEAD_DIM)
    scores = (
        jnp.einsum("tgrd,ngd->tgrn", query, suffix_keys, preferred_element_type=jnp.float32) * scale
    )
    best, total, acc = merge_block(carry, scores, suffix_values, visible[:, None, None, :])
    attended = (acc / total[..., None]).astype(jnp.bfloat16).reshape(rows, head_cols)
    projected = jnp.dot(attended, full_out, preferred_element_type=jnp.float32)
    hidden_state = (inputs.astype(jnp.float32) + projected).astype(jnp.bfloat16)
    moe_input = rms_norm(hidden_state, ffn_gain)
    total_units = expert_in.shape[0] * lanes
    parts = total_units // EXPERTS
    unit_ff = expert_in.shape[2] // 2
    flat_ids = expert_ids[0].reshape(-1)
    onehot = (flat_ids[:, None] == jnp.arange(EXPERTS, dtype=jnp.int32)[None, :]).astype(jnp.int32)
    earlier_count = jnp.cumsum(onehot, axis=0, dtype=jnp.int32) - onehot
    slots = jnp.sum(earlier_count * onehot, axis=1, dtype=jnp.int32)
    unit_ids = flat_ids[:, None] * parts + jnp.arange(parts, dtype=jnp.int32)[None, :]
    target = (unit_ids * CAP + slots[:, None]).reshape(-1)
    row_of = jnp.repeat(jnp.arange(rows, dtype=jnp.int32), TOPK * parts)
    source = jnp.full((total_units * CAP,), rows, jnp.int32).at[target].set(row_of)
    padded_input = jnp.concatenate([moe_input, jnp.zeros((1, model), jnp.bfloat16)], axis=0)
    outgoing = padded_input[source]
    arrived = lax.all_to_all(
        outgoing.reshape(total_units, CAP, model), "tensor", split_axis=0, concat_axis=1, tiled=True
    )
    inner = jnp.einsum("erd,edf->erf", arrived, expert_in, preferred_element_type=jnp.float32)
    activated = (jax.nn.silu(inner[..., :unit_ff]) * inner[..., unit_ff:]).astype(jnp.bfloat16)
    produced = jnp.einsum(
        "erf,efd->erd", activated, expert_out, preferred_element_type=jnp.float32
    ).astype(jnp.bfloat16)
    returned = lax.all_to_all(produced, "tensor", split_axis=1, concat_axis=0, tiled=True)
    picked = returned.reshape(total_units * CAP, model)[target].reshape(rows, TOPK, parts, model)
    combined = jnp.einsum("tk,tksd->td", gate_weights[0], picked.astype(jnp.float32))
    mixed = (hidden_state.astype(jnp.float32) + combined).astype(jnp.bfloat16)
    return (hidden_state[None], mixed[None])


def solution(mesh):
    in_specs = (
        P("dp", "tensor", None),
        P(),
        P(None, "dp"),
        P("dp", None),
        P("dp", "tensor", None, None),
        P("dp", None),
        P(),
        P("dp", "tensor", None),
        P("dp", "tensor", None),
        P("tensor", None, None),
        P("tensor", None, None),
    )
    out_specs = (P("dp", "tensor", None), P("dp", "tensor", None))
    return jax.shard_map(shards, mesh=mesh, in_specs=in_specs, out_specs=out_specs, check_vma=False)
```

profile of v0, /device:TPU:1, one launch (start us, length us, event | category | flops | bytes accessed | tf_op | source)
XLA Modules:
  0.0 881.9 jit_solution(11526907995774648510)
XLA Ops:
  14.2 9.0 %reduce-window.19 = s32[32,8,128]{2,1,0:T(8,128)S(1)} reduce-window(s32[32,8,128]{2,1,0:T(8,128)S(1)} %fusion.61, s32[]{:T(128)} %constant.24.clone.1), window={size=1x1x128 pad=0_0x0_0x127_0}, to_apply=%region_11.12 | reduce-window | flops 4161536 | bytes 262148 | tf_op jit(solution)/shard_map/reduce-window.2
  24.5 8.1 scatter_custom_fusion
  34.4 57.4 %all-gather.9.cloned.1.call-done = bf16[1,512,2,512]{3,2,0,1:T(2,128)(2,1)} async-done(((bf16[1,8,2,512]{3,2,0,1:T(2,128)(2,1)}), bf16[1,512,2,512]{3,2,0,1:T(2,128)(2,1)}) %all-gather.9.cloned.1.call-update) | async-done | bytes 1048592 | tf_op jit(solution)/shard_map/all_gather | solution.py:112
  91.8 4.2 fusion.70
  96.0 3.5 copy.73
  99.5 3.5 copy.74
  103.0 69.1 %all-gather.5.cloned.1.call-done = bf16[1536,2560]{1,0:T(8,128)(2,1)} async-done(((bf16[1536,640]{1,0:T(8,128)(2,1)}), bf16[1536,2560]{1,0:T(8,128)(2,1)}) %all-gather.5.cloned.1.call-update) | async-done | bytes 7864336 | tf_op jit(solution)/shard_map/all_gather | solution.py:88
  172.1 4.5 convolution_convert_fusion.1
  178.5 3.9 collective-permute-start
  182.9 3.2 collective-permute-done
  187.2 3.7 collective-permute-start.1
  191.8 4.8 bitcast_reduce_fusion
  196.6 3.7 collective-permute-done.1
  203.8 2.1 copy.80
  207.0 3.7 fusion.3
  217.0 13.0 %all-gather.7.cloned.1.call-done = bf16[1536,1536]{1,0:T(8,128)(2,1)} async-done(((bf16[384,1536]{1,0:T(8,128)(2,1)}), bf16[1536,1536]{1,0:T(8,128)(2,1)}) %all-gather.7.cloned.1.call-update) | async-done | bytes 4718608 | tf_op jit(solution)/shard_map/all_gather | solution.py:89
  230.0 3.2 fusion.40
  233.5 9.5 %gather_fusion = bf16[2560,1536]{1,0:T(8,128)(2,1)} fusion(bf16[129,1536]{1,0:T(8,128)(2,1)S(1)} %concatenate.37, s32[3072]{0:T(1024)S(1)} %pad_clamp_fusion), kind=kCustom, calls=%fused_computation | custom fusion | bytes 15738880 | tf_op jit(solution)/shard_map/gather | solution.py:158
  243.0 185.6 %all_to_all.8 = bf16[64,40,1536]{2,1,0:T(8,128)(2,1)S(1)} all-to-all(bf16[64,40,1536]{2,1,0:T(8,128)(2,1)} %bitcast.167), channel_id=1, replica_groups=mesh['dp'=4,'tensor'=64] {'tensor'}, dimensions={0} | all-to-all | bytes 15728640 | tf_op jit(solution)/shard_map/all_to_all | solution.py:159
  428.6 4.2 convolution_bitcast_fusion
  432.8 2.3 fusion
  435.1 86.3 %copy.103 = bf16[1,2560,1536]{2,0,1:T(2,128)(2,1)} copy(bf16[1,2560,1536]{2,1,0:T(8,128)(2,1)S(1)} %fusion) | data formatting | bytes 15728640 | tf_op jit(solution)/shard_map/convert_element_type | solution.py:166
  522.0 51.5 %reduce.2 = bf16[2560,1536]{1,0:T(8,128)(2,1)} reduce(bf16[2560,1,1536]{2,1,0:T(2,128)(2,1)} %bitcast.165, bf16[]{:T(256)} %broadcast.284), dimensions={1}, to_apply=%bitcast.163.reduce_sub_computation | reduce | bytes 15728642
  573.5 17.7 %reshape.394 = bf16[64,2,30720]{2,1,0:T(2,128)(2,1)} reshape(bf16[2560,1536]{1,0:T(8,128)(2,1)} %reduce.2) | data formatting | bytes 15728640
  591.1 6.4 all-to-all-start.1
  597.8 174.3 %all-to-all-done.1 = bf16[64,2,30720]{2,1,0:T(2,128)(2,1)} async-done(((bf16[64,2,30720]{2,1,0:T(2,128)(2,1)}), bf16[64,2,30720]{2,1,0:T(2,128)(2,1)}, u32[]{:S(2)}, u32[]{:S(2)}) %all-to-all-start.1) | async-done | bytes 7864352 | tf_op jit(solution)/shard_map/all_to_all | solution.py:167
  772.1 38.0 %reshape.395 = bf16[2560,1,1536]{2,1,0:T(2,128)(2,1)} reshape(bf16[64,2,30720]{2,1,0:T(2,128)(2,1)} %all-to-all-done.1) | data formatting | bytes 15728640
  810.1 10.8 %copy.102 = bf16[1,2560,1536]{2,1,0:T(8,128)(2,1)} copy(bf16[1,2560,1536]{2,0,1:T(2,128)(2,1)} %bitcast.166) | data formatting | bytes 15728640
  820.9 17.5 %gather_fusion.1 = bf16[2048,1536]{1,0:T(8,128)(2,1)} fusion(bf16[2560,1536]{1,0:T(8,128)(2,1)} %bitcast.164, s32[2048]{0:T(1024)S(1)} %broadcast_clamp_fusion), kind=kCustom, calls=%fused_computation.1 | custom fusion | bytes 12591104 | tf_op jit(solution)/shard_map/gather | solution.py:168
  838.4 14.1 %reshape.358 = f32[128,8,2,1536]{3,2,1,0:T(2,128)} reshape(bf16[2048,1536]{1,0:T(8,128)(2,1)} %gather_fusion.1) | data formatting | bytes 18874368 | tf_op jit(solution)/shard_map/convert_element_type | solution.py:169
  852.6 18.9 %reduce_sum.89 = bf16[128,8,1536]{2,1,0:T(8,128)(2,1)} reduce(f32[128,8,2,1536]{3,2,1,0:T(2,128)} %reshape.358, f32[]{:T(128)} %constant.19.clone.1), dimensions={2}, to_apply=%region_15.16 | reduce | flops 1572864 | bytes 15728644 | tf_op jit(solution)/shard_map/tk,tksd->td/reduce_sum | solution.py:169
  871.4 2.8 fusion.72
  (107 shorter events, 26.7 us)
Async XLA Ops:
  7.2 421.4 %copy-start = (bf16[1,1536,512]{2,1,0:T(8,128)(2,1)S(1)}, bf16[1,1536,512]{2,1,0:T(8,128)(2,1)}, u32[]{:S(2)}) copy-start(bf16[1,1536,512]{2,1,0:T(8,128)(2,1)} %param.20) | copy-start | bytes 4718596
  7.2 84.6 %all-gather.9.cloned.1.call-start = ((), (), s32[]{:S(2)}) async-start(), calls=%async_computation.4 | async-start | bytes 1064960 | tf_op jit(solution)/shard_map/all_gather | solution.py:112
  7.9 164.2 %all-gather.5.cloned.1.call-start = ((), (), s32[]{:S(2)}) async-start(), calls=%async_computation.2 | async-start | bytes 9830400 | tf_op jit(solution)/shard_map/all_gather | solution.py:88
  8.7 163.5 %copy-start.2 = (bf16[1,128,1536]{2,1,0:T(8,128)(2,1)S(1)}, bf16[1,128,1536]{2,1,0:T(8,128)(2,1)}, u32[]{:S(2)}) copy-start(bf16[1,128,1536]{2,1,0:T(8,128)(2,1)} %param.11) | copy-start | bytes 1179652
  8.7 163.4 %copy-start.8 = (f32[1536]{0:T(1024)S(1)}, f32[1536]{0:T(1024)}, u32[]{:S(2)}) copy-start(f32[1536]{0:T(1024)} %param.12) | copy-start | bytes 18436
  8.7 221.3 %all-gather.7.cloned.1.call-start = ((), (), s32[]{:S(2)}) async-start(), calls=%async_computation.3 | async-start | bytes 5898240 | tf_op jit(solution)/shard_map/all_gather | solution.py:89
  24.4 8.2 copy-start.9
  34.2 68.8 %copy-start.7 = (f32[128,64]{0,1:T(8,128)}, f32[128,64]{0,1:T(8,128)S(1)}, u32[]{:S(2)}) copy-start(f32[128,64]{0,1:T(8,128)S(1)} %get-tuple-element.27) | copy-start | bytes 98308
  178.5 7.5 collective-permute-start
  187.2 13.1 %collective-permute-start.1 = (bf16[2,128,2,512]{3,1,2,0:T(8,128)(2,1)S(1)}, bf16[2,128,2,512]{3,1,2,0:T(8,128)(2,1)S(1)}, u32[]{:S(2)}, u32[]{:S(2)}) collective-permute-start(bf16[2,128,2,512]{3,1,2,0:T(8,128)(2,1)S(1)} %pad_maximum_fusion.1), channel_id=1, source_target_pairs={{0,2},{1,3},{2,4},{3,5},{4,6},{5,7},{6,8},{7,9},{8,10},{9,11},{10,... | collective-permute-start | bytes 1572872 | tf_op jit(solution)/shard_map/ppermute | solution.py:20
  191.8 14.1 %copy-start.4 = (pred[128,512]{0,1:T(8,128)(4,1)S(1)}, pred[128,512]{0,1:T(8,128)(4,1)}, u32[]{:S(2)}) copy-start(pred[128,512]{0,1:T(8,128)(4,1)} %compare_and_fusion) | copy-start | bytes 196612
  207.0 5.3 copy-start.6
  212.2 2.4 slice-start
  212.3 2.4 copy-start.5
  212.3 3.0 slice-start.1
  215.3 18.0 %copy-start.11 = (f32[1536]{0:T(1024)S(1)}, f32[1536]{0:T(1024)}, u32[]{:S(2)}) copy-start(f32[1536]{0:T(1024)} %param.17) | copy-start | bytes 18436
  233.2 641.1 %copy-start.3 = (bf16[128,1536]{1,0:T(8,128)(2,1)}, bf16[128,1536]{1,0:T(8,128)(2,1)S(1)}, u32[]{:S(2)}) copy-start(bf16[128,1536]{1,0:T(8,128)(2,1)S(1)} %get-tuple-element.26) | copy-start | bytes 1179652
  428.6 4.3 copy-start.13
  591.1 6.4 copy-start.12
  591.1 6.6 copy-start.10
  591.1 181.0 %all-to-all-start.1 = ((bf16[64,2,30720]{2,1,0:T(2,128)(2,1)}), bf16[64,2,30720]{2,1,0:T(2,128)(2,1)}, u32[]{:S(2)}, u32[]{:S(2)}) async-start(bf16[64,2,30720]{2,1,0:T(2,128)(2,1)} %reshape.394), calls=%async_computation.1 | async-start | bytes 15728640 | tf_op jit(solution)/shard_map/all_to_all | solution.py:167
  852.6 22.6 %copy-start.1 = (bf16[1,1536,512]{2,1,0:T(8,128)(2,1)S(1)}, bf16[1,1536,512]{2,1,0:T(8,128)(2,1)}, u32[]{:S(2)}) copy-start(bf16[1,1536,512]{2,1,0:T(8,128)(2,1)} %param.20) | copy-start | bytes 4718596
Sparse Core Ops, SparseCore 0:
  10.8 80.9 all-gather.8
  93.6 78.4 all-gather.4
  173.9 56.0 all-gather.6
where the time goes:
time: 890 us; the launch traced here: 882 us
  waiting for transfers between devices  323 us (36%)
  local copies, waits for them, and re-layouts  222 us (25%)
  blocking collectives  186 us (21%)
  other arithmetic  96.3 us (11%)
  matrix products  26.4 us (3%)
  between operations  14.5 us (2%)
  starting transfers between devices  14.1 us (2%)
    all_to_all x1, blocking collectives, shards(): lax.all_to_all(outgoing.reshape(total_units, CAP, model), 'tensor', split...  186 us
    all_to_all x1, waiting for transfers between devices, shards(): lax.all_to_all(produced, 'tensor', split_axis=1, concat_axis=0, tiled=True)  174 us
    convert_element_type x1, local copies, waits for them, and re-layouts, shards(): produced = jnp.einsum('erf,efd->erd', activated, expert_out, preferred_el...  86.3 us
    all_gather x1, waiting for transfers between devices, shards(): lax.all_gather(qkv_weight, 'dp', axis=1, tiled=True)  69.1 us
    unnamed x37, local copies, waits for them, and re-layouts  69.1 us
    all_gather x1, waiting for transfers between devices, shards(): piece = lax.all_gather(prefix_cache[0], 'tensor', axis=0, tiled=True)  57.4 us
    unnamed x2, other arithmetic  51.5 us
    reduce_sum x1, other arithmetic, shards(): jnp.einsum('tk,tksd->td', gate_weights[0], picked.astype(jnp.float32))  18.9 us
  transfers between devices with their start and end apart: 6, of which 6 were waited for; matrix products, arithmetic and copies ran while one was open for 7% of the time, Pallas kernels for 0%

commit v1 on v0

--- a/solution.py
+++ b/solution.py
@@ -12,6 +12,25 @@
 CAP = 40
 EPS = 1e-06
 THETA = 10000.0
+
+
+def collect(x, axis, dim):
+    size, index, span = (lax.axis_size(axis), lax.axis_index(axis), x.shape[dim])
+    forward = [(i, (i + 1) % size) for i in range(size)]
+    left = [(i, (i - 1) % size) for i in range(size)]
+    out = jnp.zeros((*x.shape[:dim], size * span, *x.shape[dim + 1 :]), x.dtype)
+    out = lax.dynamic_update_slice_in_dim(out, x, index * span, axis=dim)
+    from_left = from_right = x
+    halfway = size // 2
+    for lap in range(1, halfway + 1):
+        from_left = lax.ppermute(from_left, axis, forward)
+        out = lax.dynamic_update_slice_in_dim(out, from_left, (index - lap) % size * span, axis=dim)
+        if lap < size - halfway:
+            from_right = lax.ppermute(from_right, axis, left)
+            out = lax.dynamic_update_slice_in_dim(
+                out, from_right, (index + lap) % size * span, axis=dim
+            )
+    return out
 
 
 def from_behind(value, axis, steps):
@@ -85,7 +104,7 @@
     inputs = tokens[0]
     normed = rms_norm(inputs, attn_gain)
     full_qkv, full_out = (
-        lax.all_gather(qkv_weight, "dp", axis=1, tiled=True),
+        collect(qkv_weight, "dp", 1),
         lax.all_gather(out_weight, "dp", axis=0, tiled=True),
     )
     qkv = jnp.dot(normed, full_qkv, preferred_element_type=jnp.float32).astype(jnp.bfloat16)

time: 890 us -> 816 us (0.917)
  waiting for transfers between devices: 323 us -> 208 us
  local copies, waits for them, and re-layouts: 222 us -> 244 us
  other arithmetic: 96.3 us -> 107 us
    all_gather x1 -> x0, waiting for transfers between devices: 69.1 us -> none  [shards(): lax.all_gather(qkv_weight, 'dp', axis=1, tiled=True)]
    all_gather x1, waiting for transfers between devices: 57.4 us -> 19.8 us  [shards(): piece = lax.all_gather(prefix_cache[0], 'tensor', axis=0, tiled=True)]
    all_gather x1, waiting for transfers between devices: 13 us -> 0.02 us  [shards(): lax.all_gather(out_weight, 'dp', axis=0, tiled=True)]
    dynamic_update_slice x0 -> x4, local copies, waits for them, and re-layouts: none -> 11 us  [the longest x2 6.36 us: collect(): lax.dynamic_update_slice_in_dim(out, from_left, (index - lap) % size * sp...]
    unnamed x37 -> x43, local copies, waits for them, and re-layouts: 69.1 us -> 69.1 us
  transfers between devices with their start and end apart: 6 -> 8, of which waited for: 6 -> 5; matrix products, arithmetic and copies ran while one was open for 7% -> 12% of each run, Pallas kernels for 0% -> 0%
where the time goes in v1:
time: 816 us; the launch traced here: 805 us
  local copies, waits for them, and re-layouts  244 us (30%)
  waiting for transfers between devices  208 us (25%)
  blocking collectives  188 us (23%)
  other arithmetic  107 us (13%)
  matrix products  26.5 us (3%)
  starting transfers between devices  18.4 us (2%)
  between operations  14.7 us (2%)
    all_to_all x1, blocking collectives, shards(): lax.all_to_all(outgoing.reshape(total_units, CAP, model), 'tensor', split...  188 us
    all_to_all x1, waiting for transfers between devices, shards(): lax.all_to_all(produced, 'tensor', split_axis=1, concat_axis=0, tiled=True)  174 us
    convert_element_type x1, local copies, waits for them, and re-layouts, shards(): produced = jnp.einsum('erf,efd->erd', activated, expert_out, preferred_el...  86.3 us
    unnamed x43, local copies, waits for them, and re-layouts  69.1 us
    unnamed x2, other arithmetic  51.5 us
    all_gather x1, waiting for transfers between devices, shards(): piece = lax.all_gather(prefix_cache[0], 'tensor', axis=0, tiled=True)  19.8 us
    reduce_sum x1, other arithmetic, shards(): jnp.einsum('tk,tksd->td', gate_weights[0], picked.astype(jnp.float32))  18.9 us
    gather x1, local copies, waits for them, and re-layouts, shards(): returned.reshape(total_units * CAP, model)[target]  17.5 us
  transfers between devices with their start and end apart: 8, of which 5 were waited for; matrix products, arithmetic and copies ran while one was open for 12% of the time, Pallas kernels for 0%

profile of v1, /device:TPU:1, one launch (start us, length us, event | category | flops | bytes accessed | tf_op | source)
XLA Modules:
  0.0 805.0 jit_solution(10916416039320408288)
XLA Ops:
  14.6 9.0 %reduce-window.19 = s32[32,8,128]{2,1,0:T(8,128)S(1)} reduce-window(s32[32,8,128]{2,1,0:T(8,128)S(1)} %fusion.61, s32[]{:T(128)} %constant.38.clone.1), window={size=1x1x128 pad=0_0x0_0x127_0}, to_apply=%region_11.12 | reduce-window | flops 4161536 | bytes 262148 | tf_op jit(solution)/shard_map/reduce-window.2
  33.6 8.8 %scatter_custom_fusion = s32[2560]{0:T(1024)} fusion(s32[2048]{0:T(1024)} %bitcast.187, s32[2048]{0:T(1024)} %reshape.379, s32[]{:T(128)} %constant.86.clone.1), kind=kCustom, calls=%fused_computation.93 | custom fusion | bytes 10752 | tf_op jit(solution)/shard_map/scatter | solution.py:175
  47.1 5.4 collective-permute-done
  60.7 3.7 broadcast_in_dim.51
  65.9 3.1 constant_dynamic-update-slice_fusion.2
  68.9 3.1 constant_dynamic-update-slice_fusion.1
  72.0 19.8 %all-gather.6.cloned.1.call-done = bf16[1,512,2,512]{3,2,0,1:T(2,128)(2,1)} async-done(((bf16[1,8,2,512]{3,2,0,1:T(2,128)(2,1)}), bf16[1,512,2,512]{3,2,0,1:T(2,128)(2,1)}) %all-gather.6.cloned.1.call-update) | async-done | bytes 1048592 | tf_op jit(solution)/shard_map/all_gather | solution.py:131
  91.8 4.4 fusion.70
  96.2 3.5 copy.73
  99.7 3.5 copy.74
  103.3 3.3 constant_dynamic-update-slice_fusion
  106.6 4.5 convolution_convert_fusion.1
  116.1 3.2 collective-permute-done.3
  120.4 4.1 collective-permute-start.4
  125.4 4.8 bitcast_reduce_fusion
  130.2 4.1 collective-permute-done.4
  140.9 3.7 fusion.3
  150.8 3.2 fusion.40
  154.3 9.5 %gather_fusion = bf16[2560,1536]{1,0:T(8,128)(2,1)} fusion(bf16[129,1536]{1,0:T(8,128)(2,1)S(1)} %concatenate.37, s32[3072]{0:T(1024)S(1)} %pad_clamp_fusion), kind=kCustom, calls=%fused_computation | custom fusion | bytes 15738880 | tf_op jit(solution)/shard_map/gather | solution.py:177
  163.9 187.6 %all_to_all.8 = bf16[64,40,1536]{2,1,0:T(8,128)(2,1)S(1)} all-to-all(bf16[64,40,1536]{2,1,0:T(8,128)(2,1)} %bitcast.167), channel_id=1, replica_groups=mesh['dp'=4,'tensor'=64] {'tensor'}, dimensions={0} | all-to-all | bytes 15728640 | tf_op jit(solution)/shard_map/all_to_all | solution.py:178
  351.4 4.2 convolution_bitcast_fusion
  358.0 86.3 %copy.103 = bf16[1,2560,1536]{2,0,1:T(2,128)(2,1)} copy(bf16[1,2560,1536]{2,1,0:T(8,128)(2,1)S(1)} %fusion) | data formatting | bytes 15728640 | tf_op jit(solution)/shard_map/convert_element_type | solution.py:185
  444.8 51.5 %reduce.2 = bf16[2560,1536]{1,0:T(8,128)(2,1)} reduce(bf16[2560,1,1536]{2,1,0:T(2,128)(2,1)} %bitcast.165, bf16[]{:T(256)} %broadcast.287), dimensions={1}, to_apply=%bitcast.163.reduce_sub_computation | reduce | bytes 15728642
  496.3 17.7 %reshape.394 = bf16[64,2,30720]{2,1,0:T(2,128)(2,1)} reshape(bf16[2560,1536]{1,0:T(8,128)(2,1)} %reduce.2) | data formatting | bytes 15728640
  514.0 6.4 all-to-all-start.1
  520.6 174.3 %all-to-all-done.1 = bf16[64,2,30720]{2,1,0:T(2,128)(2,1)} async-done(((bf16[64,2,30720]{2,1,0:T(2,128)(2,1)}), bf16[64,2,30720]{2,1,0:T(2,128)(2,1)}, u32[]{:S(2)}, u32[]{:S(2)}) %all-to-all-start.1) | async-done | bytes 7864352 | tf_op jit(solution)/shard_map/all_to_all | solution.py:186
  694.9 38.0 %reshape.395 = bf16[2560,1,1536]{2,1,0:T(2,128)(2,1)} reshape(bf16[64,2,30720]{2,1,0:T(2,128)(2,1)} %all-to-all-done.1) | data formatting | bytes 15728640
  732.9 10.8 %copy.102 = bf16[1,2560,1536]{2,1,0:T(8,128)(2,1)} copy(bf16[1,2560,1536]{2,0,1:T(2,128)(2,1)} %bitcast.166) | data formatting | bytes 15728640
  743.7 17.5 %gather_fusion.1 = bf16[2048,1536]{1,0:T(8,128)(2,1)} fusion(bf16[2560,1536]{1,0:T(8,128)(2,1)} %bitcast.164, s32[2048]{0:T(1024)S(1)} %broadcast_clamp_fusion), kind=kCustom, calls=%fused_computation.1 | custom fusion | bytes 12591104 | tf_op jit(solution)/shard_map/gather | solution.py:187
  761.3 14.1 %reshape.358 = f32[128,8,2,1536]{3,2,1,0:T(2,128)} reshape(bf16[2048,1536]{1,0:T(8,128)(2,1)} %gather_fusion.1) | data formatting | bytes 18874368 | tf_op jit(solution)/shard_map/convert_element_type | solution.py:188
  775.4 18.9 %reduce_sum.89 = bf16[128,8,1536]{2,1,0:T(8,128)(2,1)} reduce(f32[128,8,2,1536]{3,2,1,0:T(2,128)} %reshape.358, f32[]{:T(128)} %constant.32.clone.1), dimensions={2}, to_apply=%region_15.16 | reduce | flops 1572864 | bytes 15728644 | tf_op jit(solution)/shard_map/tk,tksd->td/reduce_sum | solution.py:188
  794.3 2.8 fusion.72
  (121 shorter events, 55.4 us)
Async XLA Ops:
  7.2 344.3 %copy-start = (bf16[1,1536,512]{2,1,0:T(8,128)(2,1)S(1)}, bf16[1,1536,512]{2,1,0:T(8,128)(2,1)}, u32[]{:S(2)}) copy-start(bf16[1,1536,512]{2,1,0:T(8,128)(2,1)} %param.20) | copy-start | bytes 4718596
  7.2 84.6 %all-gather.6.cloned.1.call-start = ((), (), s32[]{:S(2)}) async-start(), calls=%async_computation.3 | async-start | bytes 1064960 | tf_op jit(solution)/shard_map/all_gather | solution.py:131
  7.9 142.9 %all-gather.4.cloned.1.call-start = ((), (), s32[]{:S(2)}) async-start(), calls=%async_computation.2 | async-start | bytes 5898240 | tf_op jit(solution)/shard_map/all_gather | solution.py:108
  8.0 44.6 %collective-permute-start = (bf16[1536,640]{1,0:T(8,128)(2,1)}, bf16[1536,640]{1,0:T(8,128)(2,1)}, u32[]{:S(2)}, u32[]{:S(2)}) collective-permute-start(bf16[1536,640]{1,0:T(8,128)(2,1)} %param.13), channel_id=1, source_target_pairs={{0,64},{64,128},{128,192},{192,0},{1,65},{65,129},{129,193},{193,1... | collective-permute-start | bytes 5898248 | tf_op jit(solution)/shard_map/ppermute | solution.py:26
  10.2 58.8 %collective-permute-start.1 = (bf16[1536,640]{1,0:T(8,128)(2,1)}, bf16[1536,640]{1,0:T(8,128)(2,1)}, u32[]{:S(2)}, u32[]{:S(2)}) collective-permute-start(bf16[1536,640]{1,0:T(8,128)(2,1)} %param.13), channel_id=1, source_target_pairs={{0,192},{64,0},{128,64},{192,128},{1,193},{65,1},{129,65},{193,129... | collective-permute-start | bytes 5898248 | tf_op jit(solution)/shard_map/ppermute | solution.py:29
  14.6 12.9 %copy-start.11 = (s32[256]{0:T(256)}, s32[256]{0:T(256)S(1)}, u32[]{:S(2)}) copy-start(s32[256]{0:T(256)S(1)} %add_bitcast_fusion.1) | copy-start | bytes 3076
  25.9 38.4 %copy-start.4 = (bf16[1536,640]{1,0:T(8,128)(2,1)S(1)}, bf16[1536,640]{1,0:T(8,128)(2,1)}, u32[]{:S(2)}) copy-start(bf16[1536,640]{1,0:T(8,128)(2,1)} %param.13) | copy-start | bytes 5898244
  25.9 1.5 copy-start.15
  52.5 50.7 %collective-permute-start.2 = (bf16[1536,640]{1,0:T(8,128)(2,1)}, bf16[1536,640]{1,0:T(8,128)(2,1)}, u32[]{:S(2)}, u32[]{:S(2)}) collective-permute-start(bf16[1536,640]{1,0:T(8,128)(2,1)} %collective-permute-done), channel_id=1, source_target_pairs={{0,64},{64,128},{128,192},{192,0},{1,65},{65,129},{129,193},{193,1... | collective-permute-start | bytes 5898248 | tf_op jit(solution)/shard_map/ppermute | solution.py:26
  72.0 34.5 %copy-start.2 = (bf16[1,128,1536]{2,1,0:T(8,128)(2,1)S(1)}, bf16[1,128,1536]{2,1,0:T(8,128)(2,1)}, u32[]{:S(2)}) copy-start(bf16[1,128,1536]{2,1,0:T(8,128)(2,1)} %param.11) | copy-start | bytes 1179652
  72.0 34.5 %copy-start.9 = (f32[1536]{0:T(1024)S(1)}, f32[1536]{0:T(1024)}, u32[]{:S(2)}) copy-start(f32[1536]{0:T(1024)} %param.12) | copy-start | bytes 18436
  72.0 34.5 %copy-start.14 = (f32[128]{0:T(128)S(1)}, f32[128]{0:T(128)}, u32[]{:S(2)}) copy-start(f32[128]{0:T(128)} %add_rsqrt_fusion.1) | copy-start | bytes 1540
  106.6 5.7 copy-start.5
  113.1 6.2 collective-permute-start.3
  120.4 13.9 %collective-permute-start.4 = (bf16[2,128,2,512]{3,1,2,0:T(8,128)(2,1)S(1)}, bf16[2,128,2,512]{3,1,2,0:T(8,128)(2,1)S(1)}, u32[]{:S(2)}, u32[]{:S(2)}) collective-permute-start(bf16[2,128,2,512]{3,1,2,0:T(8,128)(2,1)S(1)} %pad_maximum_fusion.1), channel_id=1, source_target_pairs={{0,2},{1,3},{2,4},{3,5},{4,6},{5,7},{6,8},{7,9},{8,10},{9,11},{10,... | collective-permute-start | bytes 1572872 | tf_op jit(solution)/shard_map/ppermute | solution.py:39
  125.4 14.5 %copy-start.6 = (pred[128,512]{0,1:T(8,128)(4,1)S(1)}, pred[128,512]{0,1:T(8,128)(4,1)}, u32[]{:S(2)}) copy-start(pred[128,512]{0,1:T(8,128)(4,1)} %compare_and_fusion) | copy-start | bytes 196612
  140.9 5.2 copy-start.8
  146.1 2.3 slice-start
  146.1 2.3 copy-start.7
  146.2 3.0 slice-start.1
  149.1 5.0 copy-start.12
  154.1 643.0 %copy-start.3 = (bf16[128,1536]{1,0:T(8,128)(2,1)}, bf16[128,1536]{1,0:T(8,128)(2,1)S(1)}, u32[]{:S(2)}) copy-start(bf16[128,1536]{1,0:T(8,128)(2,1)S(1)} %get-tuple-element.26) | copy-start | bytes 1179652
  351.4 4.3 copy-start.16
  514.0 6.4 copy-start.13
  514.0 6.6 copy-start.10
  514.0 180.9 %all-to-all-start.1 = ((bf16[64,2,30720]{2,1,0:T(2,128)(2,1)}), bf16[64,2,30720]{2,1,0:T(2,128)(2,1)}, u32[]{:S(2)}, u32[]{:S(2)}) async-start(bf16[64,2,30720]{2,1,0:T(2,128)(2,1)} %reshape.394), calls=%async_computation.1 | async-start | bytes 15728640 | tf_op jit(solution)/shard_map/all_to_all | solution.py:186
  775.4 22.6 %copy-start.1 = (bf16[1,1536,512]{2,1,0:T(8,128)(2,1)S(1)}, bf16[1,1536,512]{2,1,0:T(8,128)(2,1)}, u32[]{:S(2)}) copy-start(bf16[1,1536,512]{2,1,0:T(8,128)(2,1)} %param.20) | copy-start | bytes 4718596
Sparse Core Ops, SparseCore 0:
  10.8 81.0 all-gather.5
  93.6 52.3 all-gather.3
